TPU v7x, 32 devices: a whole 2x2x4 slice. The times are simulated.
32 devices in a mesh: fsdp: 4 (over z), tensor: 2 (over core), pool: 4 (over y, x).
Axes of the slice: x: 2, y: 2, z: 4, core: 2. Of those that a mesh axis runs over, the one named last changes fastest.
Arguments:
- hidden: bfloat16 [8192, 5120], P(('fsdp', 'pool'), 'tensor'), may hold values from -6 to 6
- queries: bfloat16 [8192, 5120], P(('fsdp', 'pool'), 'tensor'), may hold values from -200 to 200
- cotangent: bfloat16 [8192, 5120], P(('fsdp', 'pool'), 'tensor'), may hold values from -6 to 6
- segment: int32 [16, 512], P(('fsdp', 'pool')), may hold values from 0 to 15, never falling along the last dimension, each value on 1 to 384 neighbouring positions
- clip_mask: int32 [8192], P(('fsdp', 'pool')), may hold values 0 or 1
- rewards: float32 [256], P(('fsdp', 'pool')), may hold values from 0 to 1
- seq_order: int32 [256], P(('fsdp', 'pool')), may hold values from 0 to 255, each once
- kv_weight: float32 [5120, 2, 1024], P('fsdp', None, 'tensor'), may hold values from -0.078125 to 0.078125
- moment_one: float32 [5120, 2, 1024], P('fsdp', None, 'tensor'), may hold values from -60 to 60
- moment_two: float32 [5120, 2, 1024], P('fsdp', None, 'tensor'), may hold values from 1 to 10000
- dec_hidden: bfloat16 [128, 4, 5120], P(('fsdp', 'pool')), may hold values from -6 to 6
- dec_queries: bfloat16 [128, 4, 5120], P(('fsdp', 'pool'), None, 'tensor'), may hold values from -200 to 200
- kv_cache: bfloat16 [128, 256, 2, 1024], P(('fsdp', 'pool'), None, None, 'tensor'), may hold values from -6 to 6
- cache_len: int32 [128], P(('fsdp', 'pool')), may hold values from 1 to 256
Outputs:
- new_weight: float32 [5120, 2, 1024], P('fsdp', None, 'tensor')
- new_moment_one: float32 [5120, 2, 1024], P('fsdp', None, 'tensor')
- new_moment_two: float32 [5120, 2, 1024], P('fsdp', None, 'tensor')
- dec_out: bfloat16 [128, 4, 5120], P(('fsdp', 'pool'), None, 'tensor')
Inputs may be any that keep to these rules, and one draw needn't show every extreme that they name: `segment`: each row never falls; every sequence number of a row has 1 to 384 tokens. `seq_order`: each place once.
All inputs are finite; a program needn't handle non-finite values. No bound on the sum of `clip_mask` on one device may be relied on, other than what follows from the above.
Results may differ from a plain program's by a relative error of at most 0.014.
The roundings to bfloat16 on the way count: a program that leaves them out, or rounds other values in their place, can miss the bound.
Values may be sent and summed in bfloat16 or wider, within the bound.
No kernel may reach another device: no remote copies, remote signals or barrier semaphores. Data moves between devices by JAX's collectives and lax.ppermute only.
A program may use at most 128 MiB of HBM per device.

v0:
```python
import math
import jax
import jax.numpy as jnp
from jax import lax
from jax.sharding import PartitionSpec as P

D = 5120
QH = 40
KVH = 8
HD = 128
GROUP = 16
beta_one = 0.9
beta_two = 0.999
learn_rate = 0.001
weight_decay = 0.1
adam_epsilon = 1e-08
adam_step = 10.0
variance_floor = 0.04
masked_score = -1e30


def learner_grads(keys_values, queries, cotangent, segment, coefficient):
    block_rows = queries.shape[0]
    head_size = queries.shape[3]
    score_scale = 1.0 / math.sqrt(head_size)
    key_rows = keys_values[:, 0]
    value_rows = keys_values[:, 1]
    scores = (
        jnp.einsum("thrd,uhd->hrtu", queries, key_rows, preferred_element_type=jnp.float32)
        * score_scale
    )
    places = jnp.arange(block_rows)
    allowed = (segment[:, None] == segment[None, :]) & (places[None, :] <= places[:, None])
    scores = jnp.where(allowed, scores, masked_score)
    row_max = jnp.max(scores, axis=-1, keepdims=True)
    weights = jnp.exp(scores - row_max)
    attention = weights / jnp.sum(weights, axis=-1, keepdims=True)
    attention_low = attention.astype(jnp.bfloat16)
    upstream = (coefficient[:, None, None, None] * cotangent.astype(jnp.float32)).astype(
        jnp.bfloat16
    )
    grad_prob = jnp.einsum(
        "thrd,uhd->hrtu", upstream, value_rows, preferred_element_type=jnp.float32
    )
    row_inner = jnp.sum(attention * grad_prob, axis=-1, keepdims=True)
    grad_score = (attention * (grad_prob - row_inner) * score_scale).astype(jnp.bfloat16)
    grad_values = jnp.einsum(
        "hrtu,thrd->uhd", attention_low, upstream, preferred_element_type=jnp.float32
    )
    grad_keys = jnp.einsum(
        "hrtu,thrd->uhd", grad_score, queries, preferred_element_type=jnp.float32
    )
    return jnp.stack([grad_keys, grad_values], axis=1).astype(jnp.bfloat16)


def decode_attend(queries, cache, fresh, lengths):
    head_size = queries.shape[4]
    steps_here = queries.shape[1]
    capacity = cache.shape[1]
    score_scale = 1.0 / math.sqrt(head_size)
    cached = (
        jnp.einsum("bshqd,blhd->bshql", queries, cache[:, :, 0], preferred_element_type=jnp.float32)
        * score_scale
    )
    recent = (
        jnp.einsum("bshqd,bjhd->bshqj", queries, fresh[:, :, 0], preferred_element_type=jnp.float32)
        * score_scale
    )
    live = jnp.arange(capacity)[None, :] < lengths[:, None]
    cached = jnp.where(live[:, None, None, None, :], cached, masked_score)
    before = jnp.arange(steps_here)[None, :] <= jnp.arange(steps_here)[:, None]
    recent = jnp.where(before[None, :, None, None, :], recent, masked_score)
    row_max = jnp.maximum(
        jnp.max(cached, axis=-1, keepdims=True), jnp.max(recent, axis=-1, keepdims=True)
    )
    cached_exp = jnp.exp(cached - row_max)
    recent_exp = jnp.exp(recent - row_max)
    total = jnp.sum(cached_exp, axis=-1, keepdims=True) + jnp.sum(
        recent_exp, axis=-1, keepdims=True
    )
    cached_low = (cached_exp / total).astype(jnp.bfloat16)
    recent_low = (recent_exp / total).astype(jnp.bfloat16)
    output = jnp.einsum(
        "bshql,blhd->bshqd", cached_low, cache[:, :, 1], preferred_element_type=jnp.float32
    )
    output = output + jnp.einsum(
        "bshqj,bjhd->bshqd", recent_low, fresh[:, :, 1], preferred_element_type=jnp.float32
    )
    return output.astype(jnp.bfloat16).reshape(queries.shape[0], steps_here, -1)


def body(
    hidden,
    queries,
    cotangent,
    segment,
    clip_mask,
    rewards,
    seq_order,
    kv_weight,
    moment_one,
    moment_two,
    dec_hidden,
    dec_queries,
    kv_cache,
    cache_len,
):
    block_rows = hidden.shape[0]
    kv_width = kv_weight.shape[2]
    heads_here = kv_width // HD
    head_ratio = QH // KVH
    weight_low = kv_weight.astype(jnp.bfloat16)
    weight_full = lax.all_gather(weight_low, "fsdp", axis=0, tiled=True)
    tokens_full = lax.all_gather(hidden, "tensor", axis=1, tiled=True)
    projected = jnp.dot(
        tokens_full, weight_full.reshape(D, 2 * kv_width), preferred_element_type=jnp.float32
    )
    keys_values = projected.astype(jnp.bfloat16).reshape(block_rows, 2, heads_here, HD)
    shards = lax.axis_size("fsdp") * lax.axis_size("pool")
    groups_total = rewards.shape[0] * shards // GROUP
    group_of = seq_order // GROUP
    onehot = (group_of[:, None] == jnp.arange(groups_total, dtype=jnp.int32)[None, :]).astype(
        jnp.float32
    )
    stats = jnp.stack([rewards, rewards * rewards], axis=1)
    partial_sums = jnp.sum(onehot[:, :, None] * stats[:, None, :], axis=0)
    sums = lax.psum(partial_sums, ("fsdp", "pool"))
    mean = sums[:, 0] / GROUP
    spread = sums[:, 1] / GROUP - mean * mean
    denom = jnp.sqrt(jnp.maximum(spread, variance_floor))
    advantage = (rewards - jnp.sum(onehot * mean[None, :], axis=1)) / jnp.sum(
        onehot * denom[None, :], axis=1
    )
    local_seg = segment[0]
    member = (local_seg[:, None] == jnp.arange(rewards.shape[0], dtype=jnp.int32)[None, :]).astype(
        jnp.float32
    )
    coefficient = jnp.sum(member * advantage[None, :], axis=1) * clip_mask.astype(jnp.float32)
    query_rows = queries.reshape(block_rows, heads_here, head_ratio, HD)
    cot_rows = cotangent.reshape(block_rows, heads_here, head_ratio, HD)
    grad_kv = learner_grads(keys_values, query_rows, cot_rows, local_seg, coefficient).reshape(
        block_rows, 2 * kv_width
    )
    partial_value = jnp.einsum(
        "tc,tk->ck", tokens_full, grad_kv, preferred_element_type=jnp.float32
    )
    shard_grad = lax.psum_scatter(
        partial_value.reshape(kv_weight.shape[0] * lax.axis_size("fsdp"), 2, kv_width).astype(
            jnp.bfloat16
        ),
        "fsdp",
        scatter_dimension=0,
        tiled=True,
    ).astype(jnp.float32)
    grad = lax.psum(shard_grad, "pool")
    new_moment_one = beta_one * moment_one + (1.0 - beta_one) * grad
    new_moment_two = beta_two * moment_two + (1.0 - beta_two) * grad * grad
    first_hat = new_moment_one / (1.0 - beta_one**adam_step)
    second_hat = new_moment_two / (1.0 - beta_two**adam_step)
    new_weight = kv_weight - learn_rate * (
        first_hat / (jnp.sqrt(second_hat) + adam_epsilon) + weight_decay * kv_weight
    )
    dec_rows = dec_hidden.shape[0]
    steps_here = dec_hidden.shape[1]
    capacity = kv_cache.shape[1]
    rollout_low = new_weight.astype(jnp.bfloat16)
    columns = lax.all_to_all(dec_hidden, "fsdp", split_axis=2, concat_axis=0, tiled=True)
    piece_width = columns.shape[2]
    rollout_flat = rollout_low.reshape(piece_width, 2 * kv_width)
    product = jnp.dot(
        columns.reshape(dec_rows * lax.axis_size("fsdp") * steps_here, piece_width),
        rollout_flat,
        preferred_element_type=jnp.float32,
    )
    fresh = lax.psum_scatter(
        product.reshape(dec_rows * lax.axis_size("fsdp"), steps_here, 2 * kv_width),
        "fsdp",
        scatter_dimension=0,
        tiled=True,
    )
    fresh_low = fresh.astype(jnp.bfloat16).reshape(dec_rows, steps_here, 2, heads_here, HD)
    cache = kv_cache.reshape(dec_rows, capacity, 2, heads_here, HD)
    query_dec = dec_queries.reshape(dec_rows, steps_here, heads_here, head_ratio, HD)
    dec_out = decode_attend(query_dec, cache, fresh_low, cache_len)
    return (new_weight, new_moment_one, new_moment_two, dec_out)


def solution(mesh):
    return jax.shard_map(
        body,
        mesh=mesh,
        in_specs=(
            P(("fsdp", "pool"), "tensor"),
            P(("fsdp", "pool"), "tensor"),
            P(("fsdp", "pool"), "tensor"),
            P(("fsdp", "pool"), None),
            P(("fsdp", "pool")),
            P(("fsdp", "pool")),
            P(("fsdp", "pool")),
            P("fsdp", None, "tensor"),
            P("fsdp", None, "tensor"),
            P("fsdp", None, "tensor"),
            P(("fsdp", "pool"), None, None),
            P(("fsdp", "pool"), None, "tensor"),
            P(("fsdp", "pool"), None, None, "tensor"),
            P(("fsdp", "pool")),
        ),
        out_specs=(
            P("fsdp", None, "tensor"),
            P("fsdp", None, "tensor"),
            P("fsdp", None, "tensor"),
            P(("fsdp", "pool"), None, "tensor"),
        ),
        check_vma=False,
    )
```

profile of v0, /device:TPU:0, one launch (start us, length us, event | category | flops | bytes accessed | tf_op | source)
XLA Modules:
  0.0 871.9 jit_solution(16252023753719787070)
XLA Ops:
  7.2 6.2 convert_element_type.64
  13.5 0.7 all-gather.3.cloned.1.call-update
  14.3 3.0 copy.102
  17.3 4.4 copy.99
  21.8 0.1 multiply_reduce_fusion
  21.9 45.7 %psum.14 = f32[16,2]{0,1:T(2,128)S(1)} all-reduce(f32[16,2]{0,1:T(2,128)S(1)} %multiply_reduce_fusion), channel_id=1, replica_groups=mesh['fsdp'=4,'tensor'=2,'pool'=4] {'fsdp','pool'}, use_global_device_ids=true, to_apply=%region_3.4 | all-reduce | flops 32 | bytes 256 | tf_op jit(solution)/shard_map/psum | solution.py:127
  67.6 0.2 select_reduce_fusion.2
  67.8 0.1 select_reduce_fusion
  67.9 0.2 fusion.56
  68.1 132.7 %all-gather.5.cloned.1.call-done = bf16[5120,2,512]{2,1,0:T(2,128)(2,1)} async-done(((bf16[1280,2,512]{2,1,0:T(2,128)(2,1)}), bf16[5120,2,512]{2,1,0:T(2,128)(2,1)}) %all-gather.5.cloned.1.call-update) | async-done | bytes 10485776 | tf_op jit(solution)/shard_map/all_gather | solution.py:113
  200.8 12.6 %copy.142 = bf16[640,8,2,512]{3,1,2,0:T(8,128)(2,1)} copy(bf16[640,8,2,512]{3,2,1,0:T(2,128)(2,1)} %bitcast.179) | data formatting | bytes 20971520
  213.4 2.4 all-gather.3.cloned.1.call-done
  215.8 10.6 %convolution_convert_fusion.1 = bf16[512,1024]{1,0:T(8,128)(2,1)} fusion(bf16[512,5120]{1,0:T(8,128)(2,1)} %all-gather.3.cloned.1.call-done, bf16[5120,1024]{1,0:T(8,128)(2,1)} %bitcast.180), kind=kOutput, calls=%fused_computation.33 | convolution fusion | flops 5369233408 | bytes 16777216 | tf_op jit(solution)/shard_map/dot_general | solution.py:115
  226.4 2.6 reshape.138
  229.0 1.6 fusion.75
  230.6 8.5 fusion.18
  239.0 13.0 %fusion.77 = (f32[4,5,512]{2,1,0:T(8,128)S(1)}, f32[4,5,512,512]{2,3,1,0:T(8,128)}) fusion(pred[512,512]{0,1:T(8,128)(4,1)S(1)} %fusion.56, bf16[512,4,5,128]{0,3,2,1:T(8,128)(2,1)} %bitcast.187, bf16[512,1,4,128]{3,2,1,0:T(4,128)(2,1)S(1)} %get-tuple-element.27), kind=kOutput, calls=%fused_computation.99 | convolution fusion | flops 1363149312 | bytes 24420352 | tf_op jit(solution)/shard_map/sub | solution.py:36
  252.1 8.9 %fusion.43 = bf16[512,1,4,128]{0,3,2,1:T(8,128)(2,1)S(1)} fusion(bf16[512,4,5,128]{0,3,2,1:T(8,128)(2,1)S(1)} %bitcast.184, f32[512]{0:T(512)S(1)} %convert_multiply_fusion.1, f32[4,5,512,512]{2,3,1,0:T(8,128)} %get-tuple-element.31, f32[4,5,512]{2,1,0:T(8,128)S(1)} %get-tuple-element.30), kind=kOutput, calls=%fused_computation.41 | convolution fusion | flops 1356857344 | bytes 24160256 | tf_op jit(solution)/shard_map/hrtu,thrd->uhd/dot_general | solution.py:47
  261.0 27.9 %fusion.48 = bf16[512,1,4,128]{0,3,2,1:T(8,128)(2,1)S(1)} fusion(bf16[512,4,5,128]{0,3,2,1:T(8,128)(2,1)} %bitcast.188, f32[4,512,512,5]{2,1,3,0:T(8,128)} %fusion.18, f32[4,5,512,512]{2,3,1,0:T(8,128)} %get-tuple-element.31, f32[4,5,512]{2,1,0:T(8,128)S(1)} %get-tuple-element.30), kind=kOutput, calls=%fused_computation.42 | convolution fusion | flops 1379150336 | bytes 45129728 | tf_op jit(solution)/shard_map/hrtu,thrd->uhd/dot_general | solution.py:50
  288.9 0.1 pad_maximum_fusion
  289.0 10.8 %convolution_convert_fusion = bf16[1024,5120]{1,0:T(8,128)(2,1)} fusion(bf16[512,1024]{0,1:T(8,128)(2,1)S(1)} %bitcast.190, bf16[512,5120]{1,0:T(8,128)(2,1)} %all-gather.3.cloned.1.call-done), kind=kOutput, calls=%fused_computation.18 | convolution fusion | flops 5373952000 | bytes 16777216 | tf_op jit(solution)/shard_map/tc,tk->ck/dot_general | solution.py:144
  299.8 26.0 %copy.106 = bf16[5120,2,512]{2,1,0:T(2,128)(2,1)} copy(bf16[5120,2,512]{0,2,1:T(8,128)(2,1)} %bitcast.181) | data formatting | bytes 20971520 | tf_op jit(solution)/shard_map/convert_element_type | solution.py:148
  325.9 0.6 copy-done.7
  326.5 0.6 dynamic-slice
  327.8 357.9 %all-reduce.6.cloned.1.call-done = bf16[5120,2,512]{2,1,0:T(2,128)(2,1)} async-done(((bf16[5120,2,512]{2,1,0:T(2,128)(2,1)}), bf16[5120,2,512]{2,1,0:T(2,128)(2,1)}) %all-reduce.6.cloned.1.call-update) | async-done | bytes 10485776
  685.7 6.0 dynamic-slice_convert_fusion
  691.8 5.0 copy.111
  696.7 6.9 reshape.159
  703.6 12.9 %all_to_all.15 = bf16[4,2,20480]{2,1,0:T(2,128)(2,1)S(1)} all-to-all(bf16[4,2,20480]{2,1,0:T(2,128)(2,1)S(1)} %reshape.159), channel_id=1, replica_groups=mesh['fsdp'=4,'tensor'=2,'pool'=4] {'fsdp'}, dimensions={0} | all-to-all | bytes 655360 | tf_op jit(solution)/shard_map/all_to_all | solution.py:167
  716.6 7.2 reshape.160
  723.8 6.7 copy.112
  730.6 81.1 %all-reduce.4.cloned.1.call-done = f32[1280,2,512]{2,1,0:T(2,128)} async-done(((f32[1280,2,512]{2,1,0:T(2,128)}), f32[1280,2,512]{2,1,0:T(2,128)}) %all-reduce.4.cloned.1.call-update) | async-done | bytes 5242896 | tf_op jit(solution)/shard_map/psum | solution.py:155
  811.7 22.5 %fusion.73 = (bf16[1280,2,512]{2,1,0:T(2,128)(2,1)S(1)}, f32[1280,2,512]{2,1,0:T(2,128)}, f32[1280,2,512]{2,1,0:T(2,128)}, f32[1280,2,512]{2,1,0:T(2,128)}) fusion(f32[1280,2,512]{2,1,0:T(2,128)} %param.21, f32[1280,2,512]{2,1,0:T(2,128)} %all-reduce.4.cloned.1.call-done, f32[1280,2,512]{2,1,0:T(2,128)} %param.22, f32[1280,2,512]{2,1,0:T(2,128)} %param.23), kind=kLoop, calls=%fused_computation.96 | loop fusion | flops 20971520 | bytes 39321600 | tf_op jit(solution)/shard_map/convert_element_type | solution.py:166
  834.2 0.7 copy.143
  834.9 0.5 convolution_bitcast_fusion.1
  835.4 0.1 reshape.144
  835.6 1.1 copy.113
  836.7 0.2 reshape.158
  836.9 11.1 %copy.107 = bf16[8,256,2,512]{1,3,2,0:T(8,128)(2,1)} copy(bf16[8,256,2,512]{3,2,1,0:T(2,128)(2,1)} %param.26) | data formatting | bytes 8388608 | tf_op args[12]
  848.1 2.1 fusion.78
  850.2 8.5 reduce-scatter.2.cloned.1.call-done
  858.7 0.9 convert_element_type.79
  859.7 1.3 fusion.79
  861.0 0.2 fusion.63
  861.3 0.5 fusion.57
  861.8 2.3 fusion.51
  864.1 0.4 fusion.53
  864.6 0.8 reshape.156
  (40 shorter events, 0.7 us)
Async XLA Ops:
  7.2 193.7 %all-gather.5.cloned.1.call-start = ((), (), s32[]{:S(2)}) async-start(), calls=%async_computation.3 | async-start | bytes 13107200 | tf_op jit(solution)/shard_map/all_gather | solution.py:113
  13.4 202.4 %all-gather.3.cloned.1.call-start = ((), (), s32[]{:S(2)}) async-start(), calls=%async_computation.2 | async-start | bytes 7864320 | tf_op jit(solution)/shard_map/all_gather | solution.py:114
  14.2 7.5 copy-start.4
  14.2 7.5 copy-start.6
  14.2 53.6 %copy-start.2 = (s32[1,512]{1,0:T(1,128)S(1)}, s32[1,512]{1,0:T(1,128)}, u32[]{:S(2)}) copy-start(s32[1,512]{1,0:T(1,128)} %param.17) | copy-start | bytes 6148
  14.2 53.7 %copy-start.3 = (s32[512]{0:T(512)S(1)}, s32[512]{0:T(512)}, u32[]{:S(2)}) copy-start(s32[512]{0:T(512)} %param.18) | copy-start | bytes 6148
  14.2 671.5 %all-reduce.6.cloned.1.call-start = ((), (), s32[]{:S(2)}) async-start(), calls=%async_computation.6 | async-start | bytes 20971520
  325.9 0.7 copy-start.7
  325.9 485.8 %all-reduce.4.cloned.1.call-start = ((), (), s32[]{:S(2)}) async-start(), calls=%async_computation.4 | async-start | bytes 10485760 | tf_op jit(solution)/shard_map/psum | solution.py:155
  327.8 364.0 %copy-start = (bf16[8,4,5120]{2,1,0:T(4,128)(2,1)S(1)}, bf16[8,4,5120]{2,1,0:T(4,128)(2,1)}, u32[]{:S(2)}) copy-start(bf16[8,4,5120]{2,1,0:T(4,128)(2,1)} %param.24) | copy-start | bytes 983044
  691.7 167.0 %reduce-scatter.2.cloned.1.call-start = ((), (), s32[]{:S(2)}) async-start(), calls=%async_computation.5 | async-start | bytes 655360 | tf_op jit(solution)/shard_map/reduce_scatter | solution.py:175
  834.2 2.5 copy-start.1
  835.6 12.4 %copy-start.5 = (s32[8]{0:T(128)S(1)}, s32[8]{0:T(128)}, u32[]{:S(2)}) copy-start(s32[8]{0:T(128)} %param.27) | copy-start | bytes 100
Sparse Core Ops, SparseCore 0:
  13.5 187.2 all-gather.4
  202.4 13.4 all-gather.2
  326.0 359.6 all-reduce.5
  691.8 119.8 all-reduce.3
  836.9 21.8 reduce-scatter.1
where the time goes:
time: 874 us; the launch traced here: 872 us
  waiting for transfers between devices  583 us (67%)
  local copies, waits for them, and re-layouts  91.3 us (10%)
  matrix products  86.4 us (10%)
  blocking collectives  58.7 us (7%)
  other arithmetic  37.2 us (4%)
  between operations  14.7 us (2%)
    unnamed x6, waiting for transfers between devices  359 us
    all_gather x1, waiting for transfers between devices, body(): weight_full = lax.all_gather(weight_low, 'fsdp', axis=0, tiled=True)  133 us
    psum x1, waiting for transfers between devices, body(): grad = lax.psum(shard_grad, 'pool')  81.1 us
    unnamed x27, local copies, waits for them, and re-layouts  52.8 us
    psum x1, blocking collectives, body(): sums = lax.psum(partial_sums, ('fsdp', 'pool'))  45.7 us
    dot_general x1, matrix products, learner_grads(): jnp.einsum('hrtu,thrd->uhd', grad_score, queries, preferred_element_type=...  27.9 us
    convert_element_type x1, local copies, waits for them, and re-layouts, body(): partial_value.reshape(kv_weight.shape[0] * lax.axis_size('fsdp'), 2, kv_w...  26 us
    convert_element_type x1, other arithmetic, body(): rollout_low = new_weight.astype(jnp.bfloat16)  22.5 us
  transfers between devices with their start and end apart: 5, of which 5 were waited for; matrix products, arithmetic and copies ran while one was open for 7% of the time, Pallas kernels for 0%

commit v1 on v0

--- a/solution.py
+++ b/solution.py
@@ -17,6 +17,22 @@
 adam_step = 10.0
 variance_floor = 0.04
 masked_score = -1e30
+
+
+def switch_notes(unit):
+    full_n = lax.axis_size("pool")
+
+    def regions_unite(passed, block_now):
+        if block_now >= full_n:
+            return passed
+        grid = []
+        for j in tuple(range(full_n)):
+            grid.append((j, j ^ block_now))
+        a_now = regions_unite(passed + lax.ppermute(passed, "pool", grid), 2 * block_now)
+        return a_now
+
+    right_arr = regions_unite(unit, 1)
+    return right_arr
 
 
 def learner_grads(keys_values, queries, cotangent, segment, coefficient):
@@ -152,7 +168,7 @@
         scatter_dimension=0,
         tiled=True,
     ).astype(jnp.float32)
-    grad = lax.psum(shard_grad, "pool")
+    grad = switch_notes(shard_grad)
     new_moment_one = beta_one * moment_one + (1.0 - beta_one) * grad
     new_moment_two = beta_two * moment_two + (1.0 - beta_two) * grad * grad
     first_hat = new_moment_one / (1.0 - beta_one**adam_step)

time: 874 us -> 989 us (1.13)
  waiting for transfers between devices: 583 us -> 690 us
    ppermute x0 -> x2, waiting for transfers between devices: none -> 188 us  [regions_unite(): lax.ppermute(passed, 'pool', grid)]
    psum x1 -> x0, waiting for transfers between devices: 81.1 us -> none  [body(): grad = lax.psum(shard_grad, 'pool')]
    unnamed x6 -> x5, waiting for transfers between devices: 359 us -> 359 us
  transfers between devices with their start and end apart: 5 -> 6, of which waited for: 5 -> 6; matrix products, arithmetic and copies ran while one was open for 7% -> 6% of each run, Pallas kernels for 0% -> 0%
where the time goes in v1:
time: 989 us; the launch traced here: 988 us
  waiting for transfers between devices  690 us (70%)
  local copies, waits for them, and re-layouts  91.1 us (9%)
  matrix products  86.4 us (9%)
  blocking collectives  57.7 us (6%)
  other arithmetic  44.7 us (5%)
  between operations  14.7 us (1%)
    unnamed x5, waiting for transfers between devices  359 us
    ppermute x2, waiting for transfers between devices, regions_unite(): lax.ppermute(passed, 'pool', grid)  188 us
    all_gather x1, waiting for transfers between devices, body(): weight_full = lax.all_gather(weight_low, 'fsdp', axis=0, tiled=True)  133 us
    unnamed x27, local copies, waits for them, and re-layouts  52.7 us
    psum x1, blocking collectives, body(): sums = lax.psum(partial_sums, ('fsdp', 'pool'))  45.7 us
    dot_general x1, matrix products, learner_grads(): jnp.einsum('hrtu,thrd->uhd', grad_score, queries, preferred_element_type=...  27.9 us
    convert_element_type x1, local copies, waits for them, and re-layouts, body(): partial_value.reshape(kv_weight.shape[0] * lax.axis_size('fsdp'), 2, kv_w...  26 us
    convert_element_type x1, other arithmetic, body(): rollout_low = new_weight.astype(jnp.bfloat16)  25.1 us
  transfers between devices with their start and end apart: 6, of which 6 were waited for; matrix products, arithmetic and copies ran while one was open for 6% of the time, Pallas kernels for 0%

profile of v1, /device:TPU:0, one launch (start us, length us, event | category | flops | bytes accessed | tf_op | source)
XLA Modules:
  0.0 987.6 jit_solution(6864936206732009304)
XLA Ops:
  7.2 6.2 convert_element_type.64
  13.5 0.7 all-gather.3.cloned.1.call-update
  14.3 3.0 copy.102
  17.3 4.4 copy.99
  21.9 45.7 %psum.7 = f32[16,2]{0,1:T(2,128)S(1)} all-reduce(f32[16,2]{0,1:T(2,128)S(1)} %multiply_reduce_fusion), channel_id=1, replica_groups=mesh['fsdp'=4,'tensor'=2,'pool'=4] {'fsdp','pool'}, use_global_device_ids=true, to_apply=%region_3.4 | all-reduce | flops 32 | bytes 256 | tf_op jit(solution)/shard_map/psum | solution.py:143
  67.6 0.2 select_reduce_fusion.2
  67.9 0.2 fusion.56
  68.1 132.7 %all-gather.5.cloned.1.call-done = bf16[5120,2,512]{2,1,0:T(2,128)(2,1)} async-done(((bf16[1280,2,512]{2,1,0:T(2,128)(2,1)}), bf16[5120,2,512]{2,1,0:T(2,128)(2,1)}) %all-gather.5.cloned.1.call-update) | async-done | bytes 10485776 | tf_op jit(solution)/shard_map/all_gather | solution.py:129
  200.8 12.6 %copy.142 = bf16[640,8,2,512]{3,1,2,0:T(8,128)(2,1)} copy(bf16[640,8,2,512]{3,2,1,0:T(2,128)(2,1)} %bitcast.178) | data formatting | bytes 20971520
  213.4 2.4 all-gather.3.cloned.1.call-done
  215.8 10.6 %convolution_convert_fusion.1 = bf16[512,1024]{1,0:T(8,128)(2,1)} fusion(bf16[512,5120]{1,0:T(8,128)(2,1)} %all-gather.3.cloned.1.call-done, bf16[5120,1024]{1,0:T(8,128)(2,1)} %bitcast.179), kind=kOutput, calls=%fused_computation.33 | convolution fusion | flops 5369233408 | bytes 16777216 | tf_op jit(solution)/shard_map/dot_general | solution.py:131
  226.4 2.6 reshape.138
  229.0 1.6 fusion.76
  230.6 8.5 fusion.18
  239.0 13.0 %fusion.78 = (f32[4,5,512]{2,1,0:T(8,128)S(1)}, f32[4,5,512,512]{2,3,1,0:T(8,128)}) fusion(pred[512,512]{0,1:T(8,128)(4,1)S(1)} %fusion.56, bf16[512,4,5,128]{0,3,2,1:T(8,128)(2,1)} %bitcast.187, bf16[512,1,4,128]{3,2,1,0:T(4,128)(2,1)S(1)} %get-tuple-element.27), kind=kOutput, calls=%fused_computation.100 | convolution fusion | flops 1363149312 | bytes 24420352 | tf_op jit(solution)/shard_map/sub | solution.py:52
  252.1 8.9 fusion.43
  261.0 27.9 %fusion.48 = bf16[512,1,4,128]{0,3,2,1:T(8,128)(2,1)S(1)} fusion(bf16[512,4,5,128]{0,3,2,1:T(8,128)(2,1)} %bitcast.188, f32[4,512,512,5]{2,1,3,0:T(8,128)} %fusion.18, f32[4,5,512,512]{2,3,1,0:T(8,128)} %get-tuple-element.31, f32[4,5,512]{2,1,0:T(8,128)S(1)} %get-tuple-element.30), kind=kOutput, calls=%fused_computation.42 | convolution fusion | flops 1379150336 | bytes 45129728 | tf_op jit(solution)/shard_map/hrtu,thrd->uhd/dot_general | solution.py:66
  289.0 10.8 %convolution_convert_fusion = bf16[1024,5120]{1,0:T(8,128)(2,1)} fusion(bf16[512,1024]{0,1:T(8,128)(2,1)S(1)} %bitcast.190, bf16[512,5120]{1,0:T(8,128)(2,1)} %all-gather.3.cloned.1.call-done), kind=kOutput, calls=%fused_computation.18 | convolution fusion | flops 5373952000 | bytes 16777216 | tf_op jit(solution)/shard_map/tc,tk->ck/dot_general | solution.py:160
  299.8 26.0 %copy.106 = bf16[5120,2,512]{2,1,0:T(2,128)(2,1)} copy(bf16[5120,2,512]{0,2,1:T(8,128)(2,1)} %bitcast.180) | data formatting | bytes 20971520 | tf_op jit(solution)/shard_map/convert_element_type | solution.py:164
  325.9 0.6 copy-done.7
  326.5 0.6 dynamic-slice
  327.8 357.9 %all-reduce.3.cloned.1.call-done = bf16[5120,2,512]{2,1,0:T(2,128)(2,1)} async-done(((bf16[5120,2,512]{2,1,0:T(2,128)(2,1)}), bf16[5120,2,512]{2,1,0:T(2,128)(2,1)}) %all-reduce.3.cloned.1.call-update) | async-done | bytes 10485776
  685.7 4.2 dynamic-slice_convert_fusion
  690.0 1.5 collective-permute-start
  691.5 113.1 %collective-permute-done = f32[1280,2,512]{2,1,0:T(2,128)S(1)} collective-permute-done((f32[1280,2,512]{2,1,0:T(2,128)S(1)}, f32[1280,2,512]{2,1,0:T(2,128)S(1)}, u32[]{:S(2)}, u32[]{:S(2)}) %collective-permute-start) | collective-permute-done | bytes 5242912 | tf_op jit(solution)/shard_map/ppermute | solution.py:31
  804.6 6.6 fusion.66
  811.3 1.5 collective-permute-start.1
  812.8 5.0 copy.111
  817.7 6.9 reshape.159
  824.6 12.0 %all_to_all.15 = bf16[4,2,20480]{2,1,0:T(2,128)(2,1)S(1)} all-to-all(bf16[4,2,20480]{2,1,0:T(2,128)(2,1)S(1)} %reshape.159), channel_id=1, replica_groups=mesh['fsdp'=4,'tensor'=2,'pool'=4] {'fsdp'}, dimensions={0} | all-to-all | bytes 655360 | tf_op jit(solution)/shard_map/all_to_all | solution.py:183
  836.5 7.2 reshape.160
  843.7 6.7 copy.112
  850.5 74.9 %collective-permute-done.1 = f32[1280,2,512]{2,1,0:T(2,128)} collective-permute-done((f32[1280,2,512]{2,1,0:T(2,128)}, f32[1280,2,512]{2,1,0:T(2,128)}, u32[]{:S(2)}, u32[]{:S(2)}) %collective-permute-start.1) | collective-permute-done | bytes 5242912 | tf_op jit(solution)/shard_map/ppermute | solution.py:31
  925.4 25.1 %fusion.74 = (bf16[1280,2,512]{2,1,0:T(2,128)(2,1)S(1)}, f32[1280,2,512]{2,1,0:T(2,128)}, f32[1280,2,512]{2,1,0:T(2,128)}, f32[1280,2,512]{2,1,0:T(2,128)}) fusion(f32[1280,2,512]{2,1,0:T(2,128)} %param.21, f32[1280,2,512]{2,1,0:T(2,128)} %fusion.66, f32[1280,2,512]{2,1,0:T(2,128)} %collective-permute-done.1, f32[1280,2,512]{2,1,0:T(2,128)} %param.22, ...), kind=kLoop, calls=%fused_computation.97 | loop fusion | flops 22282240 | bytes 44564480 | tf_op jit(solution)/shard_map/convert_element_type | solution.py:182
  950.4 0.7 copy.143
  951.1 0.5 convolution_bitcast_fusion.1
  951.8 1.1 copy.113
  953.0 0.2 reshape.158
  953.2 11.1 %copy.107 = bf16[8,256,2,512]{1,3,2,0:T(8,128)(2,1)} copy(bf16[8,256,2,512]{3,2,1,0:T(2,128)(2,1)} %param.26) | data formatting | bytes 8388608 | tf_op args[12]
  964.3 2.1 fusion.79
  966.5 8.0 reduce-scatter.2.cloned.1.call-done
  974.4 0.9 convert_element_type.79
  975.4 1.3 fusion.80
  976.7 0.2 fusion.63
  977.0 0.5 fusion.57
  977.5 2.3 fusion.51
  979.8 0.4 fusion.53
  980.3 0.8 reshape.156
  (42 shorter events, 1.1 us)
Async XLA Ops:
  7.2 193.7 %all-gather.5.cloned.1.call-start = ((), (), s32[]{:S(2)}) async-start(), calls=%async_computation.3 | async-start | bytes 13107200 | tf_op jit(solution)/shard_map/all_gather | solution.py:129
  13.4 202.4 %all-gather.3.cloned.1.call-start = ((), (), s32[]{:S(2)}) async-start(), calls=%async_computation.2 | async-start | bytes 7864320 | tf_op jit(solution)/shard_map/all_gather | solution.py:130
  14.2 7.5 copy-start.4
  14.2 7.5 copy-start.6
  14.2 53.6 %copy-start.2 = (s32[1,512]{1,0:T(1,128)S(1)}, s32[1,512]{1,0:T(1,128)}, u32[]{:S(2)}) copy-start(s32[1,512]{1,0:T(1,128)} %param.17) | copy-start | bytes 6148
  14.2 53.7 %copy-start.3 = (s32[512]{0:T(512)S(1)}, s32[512]{0:T(512)}, u32[]{:S(2)}) copy-start(s32[512]{0:T(512)} %param.18) | copy-start | bytes 6148
  14.2 671.5 %all-reduce.3.cloned.1.call-start = ((), (), s32[]{:S(2)}) async-start(), calls=%async_computation.5 | async-start | bytes 20971520
  325.9 0.7 copy-start.7
  325.9 648.5 %reduce-scatter.2.cloned.1.call-start = ((), (), s32[]{:S(2)}) async-start(), calls=%async_computation.4 | async-start | bytes 655360 | tf_op jit(solution)/shard_map/reduce_scatter | solution.py:191
  690.0 122.8 %copy-start = (bf16[8,4,5120]{2,1,0:T(4,128)(2,1)S(1)}, bf16[8,4,5120]{2,1,0:T(4,128)(2,1)}, u32[]{:S(2)}) copy-start(bf16[8,4,5120]{2,1,0:T(4,128)(2,1)} %param.24) | copy-start | bytes 983044
  690.0 114.7 %collective-permute-start = (f32[1280,2,512]{2,1,0:T(2,128)S(1)}, f32[1280,2,512]{2,1,0:T(2,128)S(1)}, u32[]{:S(2)}, u32[]{:S(2)}) collective-permute-start(f32[1280,2,512]{2,1,0:T(2,128)S(1)} %dynamic-slice_convert_fusion), channel_id=1, source_target_pairs={{0,1},{1,0},{2,3},{3,2},{4,5},{5,4},{6,7},{7,6},{8,9},{9,8},{10,11... | collective-permute-start | bytes 15728648 | tf_op jit(solution)/shard_map/ppermute | solution.py:31
  811.3 114.1 %collective-permute-start.1 = (f32[1280,2,512]{2,1,0:T(2,128)}, f32[1280,2,512]{2,1,0:T(2,128)}, u32[]{:S(2)}, u32[]{:S(2)}) collective-permute-start(f32[1280,2,512]{2,1,0:T(2,128)} %fusion.66), channel_id=1, source_target_pairs={{0,2},{1,3},{2,0},{3,1},{4,6},{5,7},{6,4},{7,5},{8,10},{9,11},{10,... | collective-permute-start | bytes 15728648 | tf_op jit(solution)/shard_map/ppermute | solution.py:31
  950.4 2.5 copy-start.1
  951.8 12.4 %copy-start.5 = (s32[8]{0:T(128)S(1)}, s32[8]{0:T(128)}, u32[]{:S(2)}) copy-start(s32[8]{0:T(128)} %param.27) | copy-start | bytes 100
Sparse Core Ops, SparseCore 0:
  13.5 187.2 all-gather.4
  202.4 13.4 all-gather.2
  326.0 359.6 all-reduce.2
  953.1 21.3 reduce-scatter.1
